TPU v7x, 32 devices: a whole 2x2x4 slice. The times are simulated.
32 devices in a mesh: stack: 2 (over y), acq: 4 (over z), lines: 4 (over x, core).
Axes of the slice: x: 2, y: 2, z: 4, core: 2. Of those that a mesh axis runs over, the one named last changes fastest.
Arguments:
- returned_radar_signal_data: bfloat16 [8, 2, 512, 4096], P(('stack', 'acq'), None, 'lines'), parts along dimension 0, may hold values from -6 to 6
- slant_replica_filter_response: float32 [8, 2, 4096], P(('stack', 'acq')), parts along dimension 0, may hold values from -6 to 6
- along_track_sharpening_slope: float32 [8, 4096], P(('stack', 'acq'), 'lines'), parts along dimension 0, may hold values from 0.25 to 1
- motion_shift_centroid_hz: float32 [8, 4096], P(('stack', 'acq'), 'lines'), parts along dimension 0, may hold values from -0.2 to 0.2
- valid_along_track_rows: int32 [8], P(('stack', 'acq')), parts along dimension 0, may hold values from 256 to 512, as said below
- reference_index: int32 [2], P('stack'), parts along dimension 0, may hold values from 0 to 3
- patch_offsets: int32 [8, 2, 4, 32], P(('stack', 'acq'), None, None, 'lines'), parts along dimension 0, may hold values from -64 to 64
Outputs:
- correlation: float32 [8, 2, 256, 2048], P(('stack', 'acq'), None, None, 'lines'), parts along dimension 0
There are 2 independent parts, one for each index of `stack`. A program takes and returns all parts, laid end to end along the dimension named above; each array names one. Nothing has to cross between parts.
Inputs may be any that keep to these rules, and one draw needn't show every extreme that they name: `valid_along_track_rows`: some acquisition has all 512 lines valid and some exactly half of them.
All inputs are finite; a program needn't handle non-finite values.
Results may differ from a plain program's by a relative error of at most 0.0053.
Values may be sent and summed in bfloat16 or wider, within the bound.
A program may use at most 64 MiB of HBM per device.

v0:
```python
import functools
import math

import jax
import jax.numpy as jnp
import numpy as np
from jax import lax
from jax.experimental import pallas as pl
from jax.experimental.pallas import tpu as pltpu
from jax.sharding import PartitionSpec as P

PATCH = 64
LANES = 128
eps = 1e-06
bf16 = jnp.bfloat16
f32 = jnp.float32


def dft(size, sign):
    index = np.arange(size)
    angle = 2.0 * np.pi * (np.outer(index, index) % size) / size
    return np.cos(angle) + 1j * sign * np.sin(angle)


def right_form(matrix):
    return np.block([[matrix.real, matrix.imag], [-matrix.imag, matrix.real]])


def left_form(matrix):
    return np.block([[matrix.real, -matrix.imag], [matrix.imag, matrix.real]])


def halves(matrix):
    high = np.asarray(matrix, np.float32).astype(bf16)
    low = (np.asarray(matrix, np.float64) - high.astype(np.float64)).astype(bf16)
    return np.stack([high, low])


def split(value):
    high = value.astype(bf16)
    return high, (value - high.astype(f32)).astype(bf16)


def dot(a, b):
    return jnp.dot(a, b, preferred_element_type=f32)


def fft_list(values, sign):
    count = len(values)
    if count == 1:
        return values
    even = fft_list(values[0::2], sign)
    odd = fft_list(values[1::2], sign)
    out = [None] * count
    for k in range(count // 2):
        re, im = odd[k]
        if k == 0:
            pass
        elif 4 * k == count:
            re, im = (-im, re) if sign > 0 else (im, -re)
        elif 8 * k == count:
            r = math.sqrt(0.5)
            re, im = ((re - im) * r, (re + im) * r) if sign > 0 else ((re + im) * r, (im - re) * r)
        elif 8 * k == 3 * count:
            r = math.sqrt(0.5)
            re, im = ((re + im) * -r, (re - im) * r) if sign > 0 else ((im - re) * r, (re + im) * -r)
        else:
            c = math.cos(2 * math.pi * k / count)
            s = sign * math.sin(2 * math.pi * k / count)
            re, im = re * c - im * s, re * s + im * c
        out[k] = (even[k][0] + re, even[k][1] + im)
        out[k + count // 2] = (even[k][0] - re, even[k][1] - im)
    return out


def range_body(valid_ref, echo_ref, filt_ref, tw_ref, fwd_ref, inv_ref, out_ref, zh, zl):
    rows = echo_ref.shape[2]
    lead = echo_ref.shape[3] // LANES
    first = lax.axis_index("lines") * (rows * pl.num_programs(0)) + pl.program_id(0) * rows
    group = 16

    def load(g):
        r0 = g * group
        line = first + r0 + lax.broadcasted_iota(jnp.int32, (group, 1), 0)
        keep = (line < valid_ref[0]).astype(f32)
        values = [
            tuple(
                echo_ref[0, q, r0 : r0 + group, LANES * a : LANES * a + LANES].astype(f32) * keep
                for q in range(2)
            )
            for a in range(lead)
        ]
        for c, (re, im) in enumerate(fft_list(values, -1.0)):
            tr, ti = tw_ref[0, c : c + 1, :], tw_ref[1, c : c + 1, :]
            put(c * rows + r0, group, re * tr - im * ti, re * ti + im * tr)

    def put(row, count, re, im):
        zh[row : row + count, :LANES], zl[row : row + count, :LANES] = split(re)
        zh[row : row + count, LANES:], zl[row : row + count, LANES:] = split(im)

    def product(m_ref):
        h = zh[...]
        return dot(h, m_ref[0]) + dot(zl[...], m_ref[0]) + dot(h, m_ref[1])

    for g in range(rows // group):
        load(g)
    y = product(fwd_ref)
    for c in range(lead):
        part = y[c * rows : c * rows + rows]
        re, im = part[:, :LANES], part[:, LANES:]
        hr, hi = filt_ref[0, c : c + 1, :], filt_ref[1, c : c + 1, :]
        put(c * rows, rows, re * hr - im * hi, re * hi + im * hr)
    y = product(inv_ref)
    for g in range(rows // group):
        r0 = g * group
        values = []
        for c in range(lead):
            part = y[c * rows + r0 : c * rows + r0 + group]
            re, im = part[:, :LANES], part[:, LANES:]
            tr, ti = tw_ref[0, c : c + 1, :], tw_ref[1, c : c + 1, :]
            values.append((re * tr + im * ti, im * tr - re * ti))
        for a, pair in enumerate(fft_list(values, 1.0)):
            for q in range(2):
                out_ref[q, r0 : r0 + group, LANES * a : LANES * a + LANES] = pair[q].astype(bf16)


def range_compress(valid, echo, filt):
    rows, length = echo.shape[2:]
    lead = length // LANES
    block = min(rows, 32)
    fwd = halves(right_form(dft(LANES, -1.0)))
    inv = halves(right_form(dft(LANES, 1.0)))
    angle = 2 * np.pi * np.outer(np.arange(lead), np.arange(LANES)) / length
    tw = np.stack([np.cos(angle), -np.sin(angle)]).astype(np.float32)
    filt = filt[0].reshape(2, LANES, lead).transpose(0, 2, 1) * (1.0 / length)
    whole = lambda x: pl.BlockSpec(x.shape, lambda g: (0,) * x.ndim)
    return pl.pallas_call(
        range_body,
        grid=(rows // block,),
        in_specs=[
            pl.BlockSpec(memory_space=pltpu.SMEM),
            pl.BlockSpec((1, 2, block, length), lambda g: (0, 0, g, 0)),
            whole(filt),
            whole(tw),
            whole(fwd),
            whole(inv),
        ],
        out_specs=pl.BlockSpec((2, block, length), lambda g: (0, g, 0)),
        out_shape=jax.ShapeDtypeStruct((2, rows, length), bf16),
        scratch_shapes=[pltpu.VMEM((lead * block, 2 * LANES), bf16)] * 2,
        name="range_compress",
    )(valid, echo, filt, tw, fwd, inv)


def unit_polys():
    z = 0.125 - 0.125 * np.cos(np.pi * (np.arange(400) + 0.5) / 400)
    f = np.sqrt(z)
    cosine = np.polynomial.Polynomial.fit(z, np.cos(2 * np.pi * f), 7, domain=[0, 0.25]).convert()
    sine = np.polynomial.Polynomial.fit(z, np.sin(2 * np.pi * f) / f, 6, domain=[0, 0.25]).convert()
    return [float(v) for v in cosine.coef], [float(v) for v in sine.coef]


def cos_sin_turns(turns):
    cosine, sine = unit_polys()
    frac = turns - jnp.round(turns)
    z = frac * frac

    def horner(coef):
        value = jnp.full_like(z, coef[-1])
        for v in coef[-2::-1]:
            value = value * z + v
        return value

    return horner(cosine), horner(sine) * frac


def azimuth_body(in_ref, slope_ref, centre_ref, fwd_ref, inv_ref, sel_ref, out_ref, crop_ref):
    total, cols = in_ref.shape[1:]
    lead = total // LANES
    values = [
        tuple(in_ref[q, LANES * a : LANES * a + LANES, :].astype(f32) for q in range(2))
        for a in range(lead)
    ]
    values = fft_list(values, -1.0)
    sharp = slope_ref[...] * (total / 8.0)
    centre = centre_ref[...]
    back = []
    for c in range(lead):
        h, l = split(jnp.concatenate(values[c], axis=0))
        y = dot(fwd_ref[0, c], h) + dot(fwd_ref[0, c], l) + dot(fwd_ref[1, c], h)
        k = c + lead * lax.broadcasted_iota(jnp.int32, (LANES, 1), 0)
        u = jnp.where(k >= total // 2, k - total, k).astype(f32) * (1.0 / total)
        w = u - centre
        co, si = cos_sin_turns(sharp * w * w)
        re, im = y[:LANES], y[LANES:]
        h, l = split(jnp.concatenate([re * co - im * si, re * si + im * co], axis=0))
        y = dot(inv_ref[0, c], h) + dot(inv_ref[0, c], l) + dot(inv_ref[1, c], h)
        back.append((y[:LANES], y[LANES:]))
    half = PATCH // 2
    for a, pair in enumerate(fft_list(back, 1.0)):
        for q in range(2):
            image = pair[q].astype(bf16)
            out_ref[q, LANES * a : LANES * a + LANES, :] = image
            crop = dot(image[half : half + PATCH], sel_ref[...])
            crop_ref[q, PATCH * a : PATCH * a + PATCH, :] = crop.astype(bf16)


def azimuth_focus(turned, slope, centre):
    total, cols = turned.shape[1:]
    lead = total // LANES
    block = 2 * LANES
    fwd, inv = [], []
    for c in range(lead):
        phase = np.exp(-2j * np.pi * c * np.arange(LANES) / total)
        fwd.append(left_form(dft(LANES, -1.0) * phase[None, :]))
        inv.append(left_form(dft(LANES, 1.0) * phase.conj()[:, None] / total))
    fwd, inv = halves(np.stack(fwd)), halves(np.stack(inv))
    sel = np.zeros((block, LANES), np.float32)
    lane = np.arange(PATCH)
    sel[lane + PATCH // 2, lane] = 1
    sel[lane + LANES + PATCH // 2, lane + PATCH] = 1
    sel = sel.astype(bf16)
    whole = lambda x: pl.BlockSpec(x.shape, lambda g: (0,) * x.ndim)
    column = lambda shape: pl.BlockSpec(shape, lambda g: (0,) * (len(shape) - 1) + (g,))
    return pl.pallas_call(
        azimuth_body,
        grid=(cols // block,),
        in_specs=[
            column((2, total, block)),
            column((1, block)),
            column((1, block)),
            whole(fwd),
            whole(inv),
            whole(sel),
        ],
        out_specs=[column((2, total, block)), column((2, total // 2, LANES))],
        out_shape=[
            jax.ShapeDtypeStruct((2, total, cols), bf16),
            jax.ShapeDtypeStruct((2, total // 2, cols // 2), bf16),
        ],
        name="azimuth_focus",
    )(turned, slope, centre, fwd, inv, sel)


def correlate_body(
    off_ref, image_ref, left_ref, right_ref, crop_ref, fr_ref, fl_ref, ir_ref, il_ref, ones_ref,
    out_ref, padded, stack, high, low, power,
):
    total, cols = image_ref.shape[1:]
    half = PATCH // 2
    row_blocks, pairs = total // LANES, cols // (2 * LANES)
    count = row_blocks * pairs
    for q in range(2):
        padded[q, :half, :] = jnp.zeros((half, cols + 3 * LANES), f32)
        padded[q, half + total :, :] = jnp.zeros((half + 8, cols + 3 * LANES), f32)
        padded[q, half : half + total, :LANES] = left_ref[q].astype(f32)
        padded[q, half : half + total, LANES : LANES + cols] = image_ref[q].astype(f32)
        padded[q, half : half + total, LANES + cols : 2 * LANES + cols] = right_ref[q].astype(f32)
    lane = lax.broadcasted_iota(jnp.int32, (1, LANES), 1)

    def window(q, i, j, target):
        row = LANES * i + PATCH + off_ref[0, 0, i, j]
        col = LANES * j + LANES + half + off_ref[0, 1, i, j]
        base = pl.multiple_of(col // LANES * LANES, LANES)
        offset = col - base
        shift = (target - offset + LANES) % LANES
        top = pl.multiple_of(row // 8 * 8, 8)
        first = padded[q, pl.ds(top, PATCH + 8), pl.ds(base, LANES)]
        second = padded[q, pl.ds(top, PATCH + 8), pl.ds(pl.multiple_of(base + LANES, LANES), LANES)]
        first = pltpu.roll(first, shift, 1)
        second = pltpu.roll(second, shift, 1)
        joined = jnp.where(lane + offset - target < LANES, first, second)
        return pltpu.roll(joined, (PATCH + 8 - (row - top)) % (PATCH + 8), 0)[:PATCH]

    def total_of(re, im):
        return jnp.sum(re * re + im * im, axis=0, keepdims=True)

    for i in range(row_blocks):
        for jp in range(pairs):
            n = i * pairs + jp
            parts = [
                jnp.where(lane < PATCH, window(q, i, 2 * jp, 0), window(q, i, 2 * jp + 1, PATCH))
                for q in range(2)
            ]
            power[count + n : count + n + 1, :] = total_of(*parts)
            prime = [
                crop_ref[q, PATCH * i : PATCH * i + PATCH, LANES * jp : LANES * jp + LANES]
                for q in range(2)
            ]
            power[n : n + 1, :] = total_of(prime[0].astype(f32), prime[1].astype(f32))
            for q in range(2):
                stack[PATCH * n : PATCH * n + PATCH, LANES * q : LANES * q + LANES] = prime[q]
                at = PATCH * (count + n)
                stack[at : at + PATCH, LANES * q : LANES * q + LANES] = parts[q].astype(bf16)

    y = dot(stack[...], fr_ref[0]) + dot(stack[...], fr_ref[1])
    for n in range(2 * count):
        part = y[PATCH * n : PATCH * n + PATCH]
        for q in range(2):
            h, l = split(part[:, LANES * q : LANES * q + LANES])
            high[PATCH * q : PATCH * q + PATCH, LANES * n : LANES * n + LANES] = h
            low[PATCH * q : PATCH * q + PATCH, LANES * n : LANES * n + LANES] = l

    def left(m_ref, h, l):
        return dot(m_ref[0], h) + dot(m_ref[0], l) + dot(m_ref[1], h)

    z = left(fl_ref, high[...], low[...])
    wide = count * LANES
    pr, pi, sr, si = z[:PATCH, :wide], z[PATCH:, :wide], z[:PATCH, wide:], z[PATCH:, wide:]
    cross = jnp.concatenate([pr * sr + pi * si, pi * sr - pr * si], axis=0)
    x = left(il_ref, *split(cross))
    for n in range(count):
        for q in range(2):
            h, l = split(x[PATCH * q : PATCH * q + PATCH, LANES * n : LANES * n + LANES])
            stack[PATCH * n : PATCH * n + PATCH, LANES * q : LANES * q + LANES] = h
            at = PATCH * (count + n)
            stack[at : at + PATCH, LANES * q : LANES * q + LANES] = l
    h, l = stack[: PATCH * count], stack[PATCH * count :]
    y = dot(h, ir_ref[0]) + dot(l, ir_ref[0]) + dot(h, ir_ref[1])
    means = jnp.dot(
        power[...], ones_ref[...], precision=lax.Precision.HIGHEST, preferred_element_type=f32
    )
    scale = lax.rsqrt(means + eps)
    factor = scale[:count] * scale[count:] * (1.0 / PATCH**3)
    for i in range(row_blocks):
        for jp in range(pairs):
            n = i * pairs + jp
            part = y[PATCH * n : PATCH * n + PATCH]
            for q in range(2):
                out_ref[
                    0, q, PATCH * i : PATCH * i + PATCH, LANES * jp : LANES * jp + LANES
                ] = part[:, LANES * q : LANES * q + LANES] * factor[n : n + 1, :]


def correlate(offsets, image, left, right, crop):
    total, cols = image.shape[1:]
    count = (total // LANES) * (cols // (2 * LANES))
    two = np.eye(2)
    fr = halves(right_form(np.kron(two, dft(PATCH, -1.0))))
    ir = halves(right_form(np.kron(two, dft(PATCH, 1.0))))
    fl = halves(left_form(dft(PATCH, -1.0)))
    il = halves(left_form(dft(PATCH, 1.0)))
    ones = np.kron(two, np.full((PATCH, PATCH), 1.0 / PATCH**2)).astype(np.float32)
    vmem = pl.BlockSpec(memory_space=pltpu.VMEM)
    return pl.pallas_call(
        correlate_body,
        in_specs=[pl.BlockSpec(memory_space=pltpu.SMEM)] + [vmem] * 9,
        out_specs=vmem,
        out_shape=jax.ShapeDtypeStruct((1, 2, total // 2, cols // 2), f32),
        scratch_shapes=[
            pltpu.VMEM((2, total + PATCH + 8, cols + 3 * LANES), f32),
            pltpu.VMEM((2 * count * PATCH, 2 * LANES), bf16),
            pltpu.VMEM((2 * PATCH, 2 * count * LANES), bf16),
            pltpu.VMEM((2 * PATCH, 2 * count * LANES), bf16),
            pltpu.VMEM((2 * count, LANES), f32),
        ],
        name="correlate",
    )(offsets, image, left, right, crop, fr, fl, ir, il, ones)


def on_device(echo, filt, slope, centre, valid, reference_index, offsets):
    compressed = range_compress(valid, echo, filt)
    turned = lax.all_to_all(compressed, "lines", split_axis=2, concat_axis=1, tiled=True)
    focused, crop = azimuth_focus(turned, slope, centre)
    mine = lax.axis_index("acq") == reference_index[0]
    primary = lax.psum(jnp.where(mine, crop, 0).astype(bf16), "acq")
    half = PATCH // 2
    cols = focused.shape[2]
    devices = lax.axis_size("lines")
    up = [(i, i + 1) for i in range(devices - 1)]
    before = lax.ppermute(focused[:, :, cols - half :], "lines", up)
    after = lax.ppermute(focused[:, :, :half], "lines", [(j, i) for i, j in up])
    left = jnp.pad(before, ((0, 0), (0, 0), (LANES - half, 0)))
    right = jnp.pad(after, ((0, 0), (0, 0), (0, LANES - half)))
    return correlate(offsets, focused, left, right, primary)


def solution(mesh):
    return jax.shard_map(
        on_device,
        mesh=mesh,
        in_specs=(
            P(("stack", "acq"), None, "lines", None),
            P(("stack", "acq"), None, None),
            P(("stack", "acq"), "lines"),
            P(("stack", "acq"), "lines"),
            P(("stack", "acq")),
            P("stack"),
            P(("stack", "acq"), None, None, "lines"),
        ),
        out_specs=P(("stack", "acq"), None, None, "lines"),
        check_vma=False,
    )
```

profile of v0, /device:TPU:0, one launch (start us, length us, event | category | flops | bytes accessed | tf_op | source)
XLA Modules:
  0.0 126.6 jit_solution(5047480838746394037)
XLA Ops:
  6.5 0.8 broadcast_multiply_fusion
  7.3 0.1 mul.12
  7.4 0.7 copy.22
  8.8 12.0 %range_compress.1 = bf16[2,128,4096]{2,1,0:T(8,128)(2,1)} custom-call(s32[1]{0:T(128)S(6)} %copy.26.valid_ref, bf16[1,2,128,4096]{3,2,1,0:T(8,128)(2,1)} %echo_ref.1, f32[2,32,128]{2,1,0:T(8,128)} %bitcast.9, f32[2,32,128]{2,1,0:T(8,128)} %constant.32.clone.tw_ref, bf16[2,256,256]{2,1,0:T(8,128)(2,1)} %constant.33.clone.fwd_ref, ...), custom_call_target="tpu_custom_call" | custom-call | tf_op jit(solution)/shard_map/range_compress/pallas_call | solution.py:137
  20.8 6.1 %copy.23 = bf16[2,128,4096]{1,0,2:T(2,128)(2,1)} copy(bf16[2,128,4096]{2,1,0:T(8,128)(2,1)} %range_compress.1) | data formatting | bytes 4194304 | tf_op jit(solution)/shard_map/range_compress/pallas_call | solution.py:137
  26.9 4.2 %all-to-all-start = ((bf16[2,128,4096]{1,0,2:T(2,128)(2,1)}), bf16[2,128,4096]{1,0,2:T(2,128)(2,1)S(1)}, u32[]{:S(2)}, u32[]{:S(2)}) async-start(bf16[2,128,4096]{1,0,2:T(2,128)(2,1)} %copy.23), calls=%async_computation | async-start | bytes 4194304 | tf_op jit(solution)/shard_map/all_to_all | solution.py:363
  31.2 0.0 all-reduce.4.cloned.1.call-start
  31.8 25.0 %all-to-all-done = bf16[2,128,4096]{1,0,2:T(2,128)(2,1)S(1)} async-done(((bf16[2,128,4096]{1,0,2:T(2,128)(2,1)}), bf16[2,128,4096]{1,0,2:T(2,128)(2,1)S(1)}, u32[]{:S(2)}, u32[]{:S(2)}) %all-to-all-start) | async-done | bytes 2097184 | tf_op jit(solution)/shard_map/all_to_all | solution.py:363
  56.8 3.8 %copy.24 = bf16[2,128,4,1024]{3,1,2,0:T(8,128)(2,1)} copy(bf16[2,128,4,1024]{1,0,3,2:T(2,128)(2,1)S(1)} %bitcast.7) | data formatting | bytes 4194304 | tf_op jit(solution)/shard_map/all_to_all | solution.py:363
  60.6 10.0 %azimuth_focus.1 = (bf16[2,512,1024]{2,1,0:T(8,128)(2,1)}, bf16[2,256,512]{2,1,0:T(8,128)(2,1)}) custom-call(bf16[2,512,1024]{2,1,0:T(8,128)(2,1)} %bitcast.8, f32[1,1024]{1,0:T(1,128)} %slope_ref.1, f32[1,1024]{1,0:T(1,128)} %centre_ref.1, bf16[2,4,256,256]{3,2,1,0:T(8,128)(2,1)} %constant.35.clone.fwd_ref, ...), custom_call_target="tpu_custom_call" | custom-call | tf_op jit(solution)/shard_map/azimuth_focus/pallas_call | solution.py:225
  70.6 1.9 %broadcast_select_fusion = bf16[2,256,512]{2,1,0:T(8,128)(2,1)} fusion(bf16[2,256,512]{2,1,0:T(8,128)(2,1)} %get-tuple-element.8, pred[]{:T(512)S(6)} %eq.3), kind=kLoop, calls=%fused_computation | loop fusion | flops 262144 | bytes 1048577 | tf_op jit(solution)/shard_map/jit(_where)/select_n | solution.py:366
  72.5 0.0 all-reduce.4.cloned.1.call-update
  72.5 1.2 fusion
  73.7 1.3 %collective-permute-start = (bf16[2,512,32]{2,1,0:T(8,128)(2,1)S(1)}, bf16[2,512,32]{2,1,0:T(8,128)(2,1)S(1)}, u32[]{:S(2)}, u32[]{:S(2)}) collective-permute-start(bf16[2,512,32]{2,1,0:T(8,128)(2,1)S(1)} %get-tuple-element.10), channel_id=1, source_target_pairs={{0,1},{1,2},{2,3},{4,5},{5,6},{6,7},{8,9},{9,10},{10,11},{12,13},{... | collective-permute-start | bytes 196616 | tf_op jit(solution)/shard_map/ppermute | solution.py:371
  75.0 1.3 %collective-permute-start.1 = (bf16[2,512,32]{2,1,0:T(8,128)(2,1)S(1)}, bf16[2,512,32]{2,1,0:T(8,128)(2,1)S(1)}, u32[]{:S(2)}, u32[]{:S(2)}) collective-permute-start(bf16[2,512,32]{2,1,0:T(8,128)(2,1)S(1)} %get-tuple-element.9), channel_id=1, source_target_pairs={{1,0},{2,1},{3,2},{5,4},{6,5},{7,6},{9,8},{10,9},{11,10},{13,12},{... | collective-permute-start | bytes 196616 | tf_op jit(solution)/shard_map/ppermute | solution.py:372
  76.3 0.0 collective-permute-done
  76.3 0.8 pad.8.left_ref
  77.2 1.9 %collective-permute-done.1 = bf16[2,512,32]{2,1,0:T(8,128)(2,1)S(1)} collective-permute-done((bf16[2,512,32]{2,1,0:T(8,128)(2,1)S(1)}, bf16[2,512,32]{2,1,0:T(8,128)(2,1)S(1)}, u32[]{:S(2)}, u32[]{:S(2)}) %collective-permute-start.1) | collective-permute-done | bytes 65568 | tf_op jit(solution)/shard_map/ppermute | solution.py:372
  79.1 0.8 pad.9.right_ref
  79.8 31.5 %all-reduce.4.cloned.1.call-done.crop_ref = bf16[2,256,512]{2,1,0:T(8,128)(2,1)} async-done(((bf16[2,256,512]{2,1,0:T(8,128)(2,1)}), bf16[2,256,512]{2,1,0:T(8,128)(2,1)}) %all-reduce.4.cloned.1.call-update) | async-done | bytes 524304 | tf_op jit(solution)/shard_map/psum | solution.py:366
  111.3 8.4 %correlate.1 = f32[1,2,256,512]{3,2,1,0:T(8,128)} custom-call(s32[1,2,4,8]{3,2,1,0:T(4,128)} %off_ref.1, bf16[2,512,1024]{2,1,0:T(8,128)(2,1)} %get-tuple-element.7.image_ref, bf16[2,512,128]{2,1,0:T(8,128)(2,1)} %pad.8.left_ref, bf16[2,512,128]{2,1,0:T(8,128)(2,1)} %pad.9.right_ref, bf16[2,256,512]{2,1,0:T(8,128)(2,1)} %all-reduce.4.cloned.1.call-done.crop_ref, ...), custom_call_target="tpu_custom_call" | custom-call | tf_op jit(solution)/shard_map/correlate/pallas_call | solution.py:345
Async XLA Ops:
  26.9 29.9 %all-to-all-start = ((bf16[2,128,4096]{1,0,2:T(2,128)(2,1)}), bf16[2,128,4096]{1,0,2:T(2,128)(2,1)S(1)}, u32[]{:S(2)}, u32[]{:S(2)}) async-start(bf16[2,128,4096]{1,0,2:T(2,128)(2,1)} %copy.23), calls=%async_computation | async-start | bytes 4194304 | tf_op jit(solution)/shard_map/all_to_all | solution.py:363
  31.2 80.2 %all-reduce.4.cloned.1.call-start = ((), (), s32[]{:S(2)}) async-start(), calls=%async_computation.1 | async-start | bytes 1048576 | tf_op jit(solution)/shard_map/psum | solution.py:366
  73.7 2.6 %collective-permute-start = (bf16[2,512,32]{2,1,0:T(8,128)(2,1)S(1)}, bf16[2,512,32]{2,1,0:T(8,128)(2,1)S(1)}, u32[]{:S(2)}, u32[]{:S(2)}) collective-permute-start(bf16[2,512,32]{2,1,0:T(8,128)(2,1)S(1)} %get-tuple-element.10), channel_id=1, source_target_pairs={{0,1},{1,2},{2,3},{4,5},{5,6},{6,7},{8,9},{9,10},{10,11},{12,13},{... | collective-permute-start | bytes 196616 | tf_op jit(solution)/shard_map/ppermute | solution.py:371
  75.0 4.0 %collective-permute-start.1 = (bf16[2,512,32]{2,1,0:T(8,128)(2,1)S(1)}, bf16[2,512,32]{2,1,0:T(8,128)(2,1)S(1)}, u32[]{:S(2)}, u32[]{:S(2)}) collective-permute-start(bf16[2,512,32]{2,1,0:T(8,128)(2,1)S(1)} %get-tuple-element.9), channel_id=1, source_target_pairs={{1,0},{2,1},{3,2},{5,4},{6,5},{7,6},{9,8},{10,9},{11,10},{13,12},{... | collective-permute-start | bytes 196616 | tf_op jit(solution)/shard_map/ppermute | solution.py:372
Sparse Core Ops, SparseCore 0:
  72.7 38.6 all-reduce.3
where the time goes:
time: 128 us; the launch traced here: 127 us
  waiting for transfers between devices  58.4 us (46%)
  Pallas kernels  30.4 us (24%)
  between operations  14.7 us (11%)
  local copies, waits for them, and re-layouts  13.5 us (11%)
  starting transfers between devices  6.84 us (5%)
  other arithmetic  2.64 us (2%)
    psum x1, waiting for transfers between devices, on_device(): primary = lax.psum(jnp.where(mine, crop, 0).astype(bf16), 'acq')  31.5 us
    all_to_all x1, waiting for transfers between devices, on_device(): lax.all_to_all(compressed, 'lines', split_axis=2, concat_axis=1, tiled=True)  25 us
    pallas_call x1, Pallas kernels, range_compress(): pl.pallas_call(range_body, grid=(rows // block,), in_specs=[pl.BlockSpec(...  12 us
    pallas_call x1, Pallas kernels, azimuth_focus(): pl.pallas_call(azimuth_body, grid=(cols // block,), in_specs=[column((2,...  10 us
    pallas_call x1, Pallas kernels, correlate(): pl.pallas_call(correlate_body, in_specs=[pl.BlockSpec(memory_space=pltpu....  8.39 us
    pallas_call x1, local copies, waits for them, and re-layouts, range_compress(): pl.pallas_call(range_body, grid=(rows // block,), in_specs=[pl.BlockSpec(...  6.15 us
    all_to_all x1, starting transfers between devices, on_device(): lax.all_to_all(compressed, 'lines', split_axis=2, concat_axis=1, tiled=True)  4.24 us
    all_to_all x1, local copies, waits for them, and re-layouts, on_device(): lax.all_to_all(compressed, 'lines', split_axis=2, concat_axis=1, tiled=True)  3.79 us
  transfers between devices with their start and end apart: 4, of which 3 were waited for; matrix products, arithmetic and copies ran while one was open for 2% of the time, Pallas kernels for 0%

commit v1 on v0

--- a/solution.py
+++ b/solution.py
@@ -73,83 +73,50 @@
     return out
 
 
-def range_body(valid_ref, echo_ref, filt_ref, tw_ref, fwd_ref, inv_ref, out_ref, zh, zl):
-    rows = echo_ref.shape[2]
+def range_block(r0, block, first, valid, echo_ref, filt_ref, tw_ref, fwd_ref, inv_ref, out_ref, zh, zl):
     lead = echo_ref.shape[3] // LANES
-    first = lax.axis_index("lines") * (rows * pl.num_programs(0)) + pl.program_id(0) * rows
     group = 16
 
-    def load(g):
-        r0 = g * group
-        line = first + r0 + lax.broadcasted_iota(jnp.int32, (group, 1), 0)
-        keep = (line < valid_ref[0]).astype(f32)
+    def put(row, count, re, im):
+        zh[row : row + count, :LANES], zl[row : row + count, :LANES] = split(re)
+        zh[row : row + count, LANES:], zl[row : row + count, LANES:] = split(im)
+
+    def product(m_ref):
+        h = zh[...]
+        return dot(h, m_ref[0]) + dot(zl[...], m_ref[0]) + dot(h, m_ref[1])
+
+    for g in range(block // group):
+        at = pl.multiple_of(r0 + g * group, group)
+        line = first + at + lax.broadcasted_iota(jnp.int32, (group, 1), 0)
+        keep = (line < valid).astype(f32)
         values = [
             tuple(
-                echo_ref[0, q, r0 : r0 + group, LANES * a : LANES * a + LANES].astype(f32) * keep
+                echo_ref[0, q, pl.ds(at, group), LANES * a : LANES * a + LANES].astype(f32) * keep
                 for q in range(2)
             )
             for a in range(lead)
         ]
         for c, (re, im) in enumerate(fft_list(values, -1.0)):
             tr, ti = tw_ref[0, c : c + 1, :], tw_ref[1, c : c + 1, :]
-            put(c * rows + r0, group, re * tr - im * ti, re * ti + im * tr)
-
-    def put(row, count, re, im):
-        zh[row : row + count, :LANES], zl[row : row + count, :LANES] = split(re)
-        zh[row : row + count, LANES:], zl[row : row + count, LANES:] = split(im)
-
-    def product(m_ref):
-        h = zh[...]
-        return dot(h, m_ref[0]) + dot(zl[...], m_ref[0]) + dot(h, m_ref[1])
-
-    for g in range(rows // group):
-        load(g)
+            put(c * block + g * group, group, re * tr - im * ti, re * ti + im * tr)
     y = product(fwd_ref)
     for c in range(lead):
-        part = y[c * rows : c * rows + rows]
+        part = y[c * block : c * block + block]
         re, im = part[:, :LANES], part[:, LANES:]
         hr, hi = filt_ref[0, c : c + 1, :], filt_ref[1, c : c + 1, :]
-        put(c * rows, rows, re * hr - im * hi, re * hi + im * hr)
+        put(c * block, block, re * hr - im * hi, re * hi + im * hr)
     y = product(inv_ref)
-    for g in range(rows // group):
-        r0 = g * group
+    for g in range(block // group):
+        at = pl.multiple_of(r0 + g * group, group)
         values = []
         for c in range(lead):
-            part = y[c * rows + r0 : c * rows + r0 + group]
+            part = y[c * block + g * group : c * block + g * group + group]
             re, im = part[:, :LANES], part[:, LANES:]
             tr, ti = tw_ref[0, c : c + 1, :], tw_ref[1, c : c + 1, :]
             values.append((re * tr + im * ti, im * tr - re * ti))
         for a, pair in enumerate(fft_list(values, 1.0)):
             for q in range(2):
-                out_ref[q, r0 : r0 + group, LANES * a : LANES * a + LANES] = pair[q].astype(bf16)
-
-
-def range_compress(valid, echo, filt):
-    rows, length = echo.shape[2:]
-    lead = length // LANES
-    block = min(rows, 32)
-    fwd = halves(right_form(dft(LANES, -1.0)))
-    inv = halves(right_form(dft(LANES, 1.0)))
-    angle = 2 * np.pi * np.outer(np.arange(lead), np.arange(LANES)) / length
-    tw = np.stack([np.cos(angle), -np.sin(angle)]).astype(np.float32)
-    filt = filt[0].reshape(2, LANES, lead).transpose(0, 2, 1) * (1.0 / length)
-    whole = lambda x: pl.BlockSpec(x.shape, lambda g: (0,) * x.ndim)
-    return pl.pallas_call(
-        range_body,
-        grid=(rows // block,),
-        in_specs=[
-            pl.BlockSpec(memory_space=pltpu.SMEM),
-            pl.BlockSpec((1, 2, block, length), lambda g: (0, 0, g, 0)),
-            whole(filt),
-            whole(tw),
-            whole(fwd),
-            whole(inv),
-        ],
-        out_specs=pl.BlockSpec((2, block, length), lambda g: (0, g, 0)),
-        out_shape=jax.ShapeDtypeStruct((2, rows, length), bf16),
-        scratch_shapes=[pltpu.VMEM((lead * block, 2 * LANES), bf16)] * 2,
-        name="range_compress",
-    )(valid, echo, filt, tw, fwd, inv)
+                out_ref[q, pl.ds(at, group), LANES * a : LANES * a + LANES] = pair[q].astype(bf16)
 
 
 def unit_polys():
@@ -174,16 +141,17 @@
     return horner(cosine), horner(sine) * frac
 
 
-def azimuth_body(in_ref, slope_ref, centre_ref, fwd_ref, inv_ref, sel_ref, out_ref, crop_ref):
-    total, cols = in_ref.shape[1:]
+def azimuth_block(col, in_ref, slope_ref, centre_ref, fwd_ref, inv_ref, sel_ref, out_ref, keep):
+    total = in_ref.shape[1]
     lead = total // LANES
+    at = pl.ds(col, 2 * LANES)
     values = [
-        tuple(in_ref[q, LANES * a : LANES * a + LANES, :].astype(f32) for q in range(2))
+        tuple(in_ref[q, LANES * a : LANES * a + LANES, at].astype(f32) for q in range(2))
         for a in range(lead)
     ]
     values = fft_list(values, -1.0)
-    sharp = slope_ref[...] * (total / 8.0)
-    centre = centre_ref[...]
+    sharp = slope_ref[:, at] * (total / 8.0)
+    centre = centre_ref[:, at]
     back = []
     for c in range(lead):
         h, l = split(jnp.concatenate(values[c], axis=0))
@@ -200,46 +168,256 @@
     for a, pair in enumerate(fft_list(back, 1.0)):
         for q in range(2):
             image = pair[q].astype(bf16)
-            out_ref[q, LANES * a : LANES * a + LANES, :] = image
+            out_ref[q, LANES * a : LANES * a + LANES, at] = image
             crop = dot(image[half : half + PATCH], sel_ref[...])
-            crop_ref[q, PATCH * a : PATCH * a + PATCH, :] = crop.astype(bf16)
-
-
-def azimuth_focus(turned, slope, centre):
-    total, cols = turned.shape[1:]
-    lead = total // LANES
-    block = 2 * LANES
+            keep(q, a, crop.astype(bf16))
+
+
+def focus_body(
+    names, sizes, valid_ref, root_ref, echo_ref, filt_ref, tw_ref, rf_ref, ri_ref,
+    slope_ref, centre_ref, af_ref, ai_ref, sel_ref,
+    image_ref, left_ref, right_ref, prime_ref,
+    zh, zl, comp, turned, crop, pass_up, pass_down, from_up, from_down,
+    send_sem, recv_sem, halo_send, halo_recv, up_send, up_recv, down_send, down_recv,
+):
+    here = {name: lax.axis_index(name) for name in names}
+    me, peers = here["lines"], sizes["lines"]
+    spot, stack_size = here["acq"], sizes["acq"]
+    rows = echo_ref.shape[2]
+    cols = image_ref.shape[2]
+    block = min(rows, 32)
+    blocks = rows // block
+    wide = 2 * LANES
+    parts = cols // wide
+
+    def device(axis, index):
+        return tuple(index if name == axis else here[name] for name in names)
+
+    def remote(src, dst, send, recv, axis, index):
+        return pltpu.make_async_remote_copy(
+            src_ref=src, dst_ref=dst, send_sem=send, recv_sem=recv,
+            device_id=device(axis, index), device_id_type=pl.DeviceIdType.MESH,
+        )
+
+    @pl.when(me == 0)
+    def _():
+        left_ref[...] = jnp.zeros_like(left_ref)
+
+    @pl.when(me == peers - 1)
+    def _():
+        right_ref[...] = jnp.zeros_like(right_ref)
+
+    @pl.when(spot == 0)
+    def _():
+        from_up[...] = jnp.zeros_like(from_up)
+
+    @pl.when(spot == stack_size - 1)
+    def _():
+        from_down[...] = jnp.zeros_like(from_down)
+
+    barrier = pltpu.get_barrier_semaphore()
+    targets = [("lines", (me + d) % peers) for d in range(1, peers)]
+    targets += [("acq", (spot + d) % stack_size) for d in (1, stack_size - 1)]
+    for axis, index in targets:
+        pl.semaphore_signal(
+            barrier, inc=1, device_id=device(axis, index), device_id_type=pl.DeviceIdType.MESH
+        )
+    pl.semaphore_wait(barrier, len(targets))
+
+    def exchange(d, b, j):
+        to = (me + d) % peers
+        source = pl.ds(pl.multiple_of(to * cols + j * wide, wide), wide)
+        land = pl.ds(pl.multiple_of(me * rows + b * block, block), block)
+        return remote(
+            comp.at[:, pl.ds(pl.multiple_of(b * block, block), block), source],
+            turned.at[:, land, pl.ds(pl.multiple_of(j * wide, wide), wide)],
+            send_sem.at[d - 1, b, j], recv_sem.at[d - 1, b, j], "lines", to,
+        )
+
+    order = sorted(range(1, peers), key=lambda d: -min(d, peers - d))
+
+    def send(b, j):
+        for d in order:
+            exchange(d, b, j).start()
+
+    def compress(b, carry):
+        r0 = pl.multiple_of(b * block, block)
+        range_block(
+            r0, block, me * rows, valid_ref[0], echo_ref, filt_ref, tw_ref, rf_ref, ri_ref,
+            comp, zh, zl,
+        )
+        own = pl.ds(pl.multiple_of(me * cols, wide), cols)
+        turned[:, pl.ds(pl.multiple_of(me * rows + r0, block), block), :] = comp[
+            :, pl.ds(r0, block), own
+        ]
+        send(b, 0)
+
+        @pl.when(b < blocks - 2)
+        def _():
+            lax.fori_loop(1, parts, lambda j, x: (send(b, j), x)[1], 0)
+
+        return carry
+
+    lax.fori_loop(0, blocks, compress, 0)
+
+    def send_late(j, carry):
+        for b in range(max(blocks - 2, 0), blocks):
+            send(b, j)
+        return carry
+
+    lax.fori_loop(1, parts, send_late, 0)
+    mine = root_ref[0] == spot
+
+    def chain(at, last, buffer, staged, send_sems, recv_sems, step):
+        ahead = spot + step
+        return remote(
+            staged.at[at], buffer.at[at], send_sems.at[at], recv_sems.at[at], "acq",
+            (ahead + stack_size) % stack_size,
+        )
+
+    lanes = (
+        (spot, spot == 0, spot == stack_size - 1, from_up, pass_up, up_send, up_recv, 1),
+        (
+            stack_size - 1 - spot, spot == stack_size - 1, spot == 0,
+            from_down, pass_down, down_send, down_recv, -1,
+        ),
+    )
+
+    def forward(tick):
+        for depth, opening, ending, buffer, staged, sends, recvs, step in lanes:
+            at = tick - depth
+
+            @pl.when(jnp.logical_and(at >= 0, at < parts))
+            def _():
+                copy = chain(at, None, buffer, staged, sends, recvs, step)
+
+                @pl.when(jnp.logical_not(opening))
+                def _():
+                    copy.wait_recv()
+
+                @pl.when(jnp.logical_not(ending))
+                def _():
+                    staged[at] = jnp.where(mine, crop[at], buffer[at])
+                    copy.start()
+
+    tile = lambda ref, col: ref.at[:, :, col : col + LANES]
+    to_left = remote(
+        tile(image_ref, 0), right_ref, halo_send.at[0], halo_recv.at[0],
+        "lines", (me + peers - 1) % peers,
+    )
+    to_right = remote(
+        tile(image_ref, cols - LANES), left_ref, halo_send.at[1], halo_recv.at[1],
+        "lines", (me + 1) % peers,
+    )
+
+    def focus(j, carry):
+        for d in order:
+            for b in range(blocks):
+                exchange(d, b, j).wait_recv()
+
+        def keep(q, a, value):
+            crop[j, q, PATCH * a : PATCH * a + PATCH, :] = value
+
+        azimuth_block(
+            pl.multiple_of(j * wide, wide), turned, slope_ref, centre_ref, af_ref, ai_ref,
+            sel_ref, image_ref, keep,
+        )
+        forward(j)
+        return carry
+
+    lax.fori_loop(0, parts, focus, 0)
+
+    @pl.when(me > 0)
+    def _():
+        to_left.start()
+
+    @pl.when(me < peers - 1)
+    def _():
+        to_right.start()
+
+    lax.fori_loop(parts, parts + stack_size - 1, lambda t, x: (forward(t), x)[1], 0)
+    for j in range(parts):
+        prime_ref[:, :, LANES * j : LANES * j + LANES] = jnp.where(
+            mine, crop[j], jnp.where(root_ref[0] < spot, from_up[j], from_down[j])
+        )
+
+    @pl.when(me > 0)
+    def _():
+        to_left.wait_send()
+        to_right.wait_recv()
+
+    @pl.when(me < peers - 1)
+    def _():
+        to_right.wait_send()
+        to_left.wait_recv()
+
+    for depth, opening, ending, buffer, staged, sends, recvs, step in lanes:
+
+        @pl.when(jnp.logical_not(ending))
+        def _():
+            for j in range(parts):
+                chain(j, None, buffer, staged, sends, recvs, step).wait_send()
+
+    def finish(j, carry):
+        for d in order:
+            for b in range(blocks):
+                exchange(d, b, j).wait_send()
+        return carry
+
+    lax.fori_loop(0, parts, finish, 0)
+
+
+def focus(names, sizes, valid, root, echo, filt, slope, centre):
+    rows, length = echo.shape[2:]
+    lead = length // LANES
+    block = min(rows, 32)
+    blocks = rows // block
+    total, cols = rows * sizes["lines"], slope.shape[1]
+    peers = sizes["lines"] - 1
+    wide = 2 * LANES
+    parts = cols // wide
+    rf = halves(right_form(dft(LANES, -1.0)))
+    ri = halves(right_form(dft(LANES, 1.0)))
+    angle = 2 * np.pi * np.outer(np.arange(lead), np.arange(LANES)) / length
+    tw = np.stack([np.cos(angle), -np.sin(angle)]).astype(np.float32)
+    filt = filt[0].reshape(2, LANES, lead).transpose(0, 2, 1) * (1.0 / length)
     fwd, inv = [], []
-    for c in range(lead):
+    for c in range(total // LANES):
         phase = np.exp(-2j * np.pi * c * np.arange(LANES) / total)
         fwd.append(left_form(dft(LANES, -1.0) * phase[None, :]))
         inv.append(left_form(dft(LANES, 1.0) * phase.conj()[:, None] / total))
     fwd, inv = halves(np.stack(fwd)), halves(np.stack(inv))
-    sel = np.zeros((block, LANES), np.float32)
+    sel = np.zeros((wide, LANES), np.float32)
     lane = np.arange(PATCH)
     sel[lane + PATCH // 2, lane] = 1
     sel[lane + LANES + PATCH // 2, lane + PATCH] = 1
     sel = sel.astype(bf16)
-    whole = lambda x: pl.BlockSpec(x.shape, lambda g: (0,) * x.ndim)
-    column = lambda shape: pl.BlockSpec(shape, lambda g: (0,) * (len(shape) - 1) + (g,))
+    smem, vmem = pl.BlockSpec(memory_space=pltpu.SMEM), pl.BlockSpec(memory_space=pltpu.VMEM)
+    dma = pltpu.SemaphoreType.DMA
+    chunk = pltpu.VMEM((parts, 2, total // 2, LANES), bf16)
     return pl.pallas_call(
-        azimuth_body,
-        grid=(cols // block,),
-        in_specs=[
-            column((2, total, block)),
-            column((1, block)),
-            column((1, block)),
-            whole(fwd),
-            whole(inv),
-            whole(sel),
-        ],
-        out_specs=[column((2, total, block)), column((2, total // 2, LANES))],
+        functools.partial(focus_body, names, sizes),
+        in_specs=[smem] * 2 + [vmem] * 10,
+        out_specs=[vmem] * 4,
         out_shape=[
             jax.ShapeDtypeStruct((2, total, cols), bf16),
+            jax.ShapeDtypeStruct((2, total, LANES), bf16),
+            jax.ShapeDtypeStruct((2, total, LANES), bf16),
             jax.ShapeDtypeStruct((2, total // 2, cols // 2), bf16),
         ],
-        name="azimuth_focus",
-    )(turned, slope, centre, fwd, inv, sel)
+        scratch_shapes=[
+            pltpu.VMEM((lead * block, wide), bf16),
+            pltpu.VMEM((lead * block, wide), bf16),
+            pltpu.VMEM((2, rows, length), bf16),
+            pltpu.VMEM((2, total, cols), bf16),
+        ]
+        + [chunk] * 5
+        + [dma((peers, blocks, parts))] * 2
+        + [dma((2,))] * 2
+        + [dma((parts,))] * 4,
+        compiler_params=pltpu.CompilerParams(collective_id=0, has_side_effects=True),
+        name="focus",
+    )(valid, root, echo, filt, tw, rf, ri, slope, centre, fwd, inv, sel)
 
 
 def correlate_body(
@@ -358,26 +536,18 @@
     )(offsets, image, left, right, crop, fr, fl, ir, il, ones)
 
 
-def on_device(echo, filt, slope, centre, valid, reference_index, offsets):
-    compressed = range_compress(valid, echo, filt)
-    turned = lax.all_to_all(compressed, "lines", split_axis=2, concat_axis=1, tiled=True)
-    focused, crop = azimuth_focus(turned, slope, centre)
-    mine = lax.axis_index("acq") == reference_index[0]
-    primary = lax.psum(jnp.where(mine, crop, 0).astype(bf16), "acq")
-    half = PATCH // 2
-    cols = focused.shape[2]
-    devices = lax.axis_size("lines")
-    up = [(i, i + 1) for i in range(devices - 1)]
-    before = lax.ppermute(focused[:, :, cols - half :], "lines", up)
-    after = lax.ppermute(focused[:, :, :half], "lines", [(j, i) for i, j in up])
-    left = jnp.pad(before, ((0, 0), (0, 0), (LANES - half, 0)))
-    right = jnp.pad(after, ((0, 0), (0, 0), (0, LANES - half)))
-    return correlate(offsets, focused, left, right, primary)
+def on_device(names, sizes, echo, filt, slope, centre, valid, reference_index, offsets):
+    image, left, right, primary = focus(
+        names, sizes, valid, reference_index, echo, filt, slope, centre
+    )
+    return correlate(offsets, image, left, right, primary)
 
 
 def solution(mesh):
+    names = tuple(mesh.axis_names)
+    sizes = {name: int(mesh.shape[name]) for name in names}
     return jax.shard_map(
-        on_device,
+        functools.partial(on_device, names, sizes),
         mesh=mesh,
         in_specs=(
             P(("stack", "acq"), None, "lines", None),

time: 128 us -> 69.1 us (0.54)
  waiting for transfers between devices: 58.4 us -> 0 us
  Pallas kernels: 30.4 us -> 66 us
  between operations: 14.7 us -> 1.32 us
  local copies, waits for them, and re-layouts: 13.5 us -> 0.81 us
  starting transfers between devices: 6.84 us -> 0 us
  other arithmetic: 2.64 us -> 0.77 us
    pallas_call x2 -> x1, Pallas kernels: 22 us -> 57.6 us  [focus(): pl.pallas_call(functools.partial(focus_body, names, sizes), in_specs=[sme...]
    psum x1 -> x0, waiting for transfers between devices: 31.5 us -> none  [on_device(): primary = lax.psum(jnp.where(mine, crop, 0).astype(bf16), 'acq')]
    all_to_all x1 -> x0, waiting for transfers between devices: 25 us -> none  [on_device(): lax.all_to_all(compressed, 'lines', split_axis=2, concat_axis=1, tiled=True)]
    pallas_call x1 -> x0, local copies, waits for them, and re-layouts: 6.15 us -> none  [range_compress(): pl.pallas_call(range_body, grid=(rows // block,), in_specs=[pl.BlockSpec(...]
    all_to_all x1 -> x0, starting transfers between devices: 4.24 us -> none  [on_device(): lax.all_to_all(compressed, 'lines', split_axis=2, concat_axis=1, tiled=True)]
    all_to_all x1 -> x0, local copies, waits for them, and re-layouts: 3.79 us -> none  [on_device(): lax.all_to_all(compressed, 'lines', split_axis=2, concat_axis=1, tiled=True)]
    ppermute x2 -> x0, starting transfers between devices: 2.6 us -> none  [the longest x1 1.31 us: on_device(): before = lax.ppermute(focused[:, :, cols - half:], 'lines', up)]
    ppermute x2 -> x0, waiting for transfers between devices: 1.88 us -> none  [the longest x1 1.88 us: on_device(): after = lax.ppermute(focused[:, :, :half], 'lines', [(j, i) for i, j in up])]
  transfers between devices with their start and end apart: 4 -> 0, of which waited for: 3 -> 0; matrix products, arithmetic and copies ran while one was open for 2% -> 0% of each run, Pallas kernels for 0% -> 0%
where the time goes in v1:
time: 69.1 us; the launch traced here: 68.9 us
  Pallas kernels  66 us (96%)
  between operations  1.32 us (2%)
  local copies, waits for them, and re-layouts  0.81 us (1%)
  other arithmetic  0.77 us (1%)
    pallas_call x1, Pallas kernels, focus(): pl.pallas_call(functools.partial(focus_body, names, sizes), in_specs=[sme...  57.6 us
    pallas_call x1, Pallas kernels, correlate(): pl.pallas_call(correlate_body, in_specs=[pl.BlockSpec(memory_space=pltpu....  8.4 us

profile of v1, /device:TPU:0, one launch (start us, length us, event | category | flops | bytes accessed | tf_op | source)
XLA Modules:
  0.0 68.9 jit_solution(18238302920992608172)
XLA Ops:
  1.3 0.8 %broadcast_multiply_fusion = f32[1,2,4096]{2,1,0:T(2,128)S(1)} fusion(f32[1,2,4096]{2,1,0:T(2,128)} %param.19), kind=kLoop, calls=%fused_computation | loop fusion | flops 8192 | bytes 65536 | tf_op jit(solution)/shard_map/mul | solution.py:383
  2.1 0.1 mul.12
  2.2 0.7 %copy.19 = f32[2,128,32]{1,2,0:T(8,128)} copy(f32[2,128,32]{2,1,0:T(8,128)S(1)} %mul.12) | data formatting | bytes 65536 | tf_op jit(solution)/shard_map/mul | solution.py:383
  2.9 57.6 %focus.1 = (bf16[2,512,1024]{2,1,0:T(8,128)(2,1)}, bf16[2,512,128]{2,1,0:T(8,128)(2,1)}, bf16[2,512,128]{2,1,0:T(8,128)(2,1)}, bf16[2,256,512]{2,1,0:T(8,128)(2,1)}) custom-call(s32[1]{0:T(128)S(6)} %copy.20.valid_ref, s32[1]{0:T(128)S(6)} %copy.21.root_ref, bf16[1,2,128,4096]{3,2,1,0:T(8,128)(2,1)} %echo_ref.1, f32[2,32,128]{2,1,0:T(8,128)} %bitcast.1, ...), custom_call_target="tpu_custom_call" | custom-call | tf_op jit(solution)/shard_map/focus/pallas_call | solution.py:398
  60.5 8.4 %correlate.1 = f32[1,2,256,512]{3,2,1,0:T(8,128)} custom-call(s32[1,2,4,8]{3,2,1,0:T(4,128)} %off_ref.1, bf16[2,512,1024]{2,1,0:T(8,128)(2,1)} %get-tuple-element.9.image_ref, bf16[2,512,128]{2,1,0:T(8,128)(2,1)} %get-tuple-element.10.left_ref, bf16[2,512,128]{2,1,0:T(8,128)(2,1)} %get-tuple-element.11.right_ref, ...), custom_call_target="tpu_custom_call" | custom-call | tf_op jit(solution)/shard_map/correlate/pallas_call | solution.py:523

commit v2 on v1

--- a/solution.py
+++ b/solution.py
@@ -43,6 +43,14 @@
 
 def dot(a, b):
     return jnp.dot(a, b, preferred_element_type=f32)
+
+
+def dot_nt(a, b):
+    return lax.dot_general(a, b, (((1,), (1,)), ((), ())), preferred_element_type=f32)
+
+
+def dot_tn(a, b):
+    return lax.dot_general(a, b, (((0,), (0,)), ((), ())), preferred_element_type=f32)
 
 
 def fft_list(values, sign):
@@ -73,7 +81,7 @@
     return out
 
 
-def range_block(r0, block, first, valid, echo_ref, filt_ref, tw_ref, fwd_ref, inv_ref, out_ref, zh, zl):
+def range_block(r0, block, first, valid, echo_ref, filt_ref, tw_ref, fwd_ref, out_ref, zh, zl):
     lead = echo_ref.shape[3] // LANES
     group = 16
 
@@ -81,9 +89,9 @@
         zh[row : row + count, :LANES], zl[row : row + count, :LANES] = split(re)
         zh[row : row + count, LANES:], zl[row : row + count, LANES:] = split(im)
 
-    def product(m_ref):
+    def product(mul):
         h = zh[...]
-        return dot(h, m_ref[0]) + dot(zl[...], m_ref[0]) + dot(h, m_ref[1])
+        return mul(h, fwd_ref[0]) + mul(zl[...], fwd_ref[0]) + mul(h, fwd_ref[1])
 
     for g in range(block // group):
         at = pl.multiple_of(r0 + g * group, group)
@@ -99,13 +107,13 @@
         for c, (re, im) in enumerate(fft_list(values, -1.0)):
             tr, ti = tw_ref[0, c : c + 1, :], tw_ref[1, c : c + 1, :]
             put(c * block + g * group, group, re * tr - im * ti, re * ti + im * tr)
-    y = product(fwd_ref)
+    y = product(dot)
     for c in range(lead):
         part = y[c * block : c * block + block]
         re, im = part[:, :LANES], part[:, LANES:]
         hr, hi = filt_ref[0, c : c + 1, :], filt_ref[1, c : c + 1, :]
         put(c * block, block, re * hr - im * hi, re * hi + im * hr)
-    y = product(inv_ref)
+    y = product(dot_nt)
     for g in range(block // group):
         at = pl.multiple_of(r0 + g * group, group)
         values = []
@@ -141,7 +149,7 @@
     return horner(cosine), horner(sine) * frac
 
 
-def azimuth_block(col, in_ref, slope_ref, centre_ref, fwd_ref, inv_ref, sel_ref, out_ref, keep):
+def azimuth_block(col, in_ref, slope_ref, centre_ref, fwd_ref, sel_ref, out_ref, keep):
     total = in_ref.shape[1]
     lead = total // LANES
     at = pl.ds(col, 2 * LANES)
@@ -162,7 +170,8 @@
         co, si = cos_sin_turns(sharp * w * w)
         re, im = y[:LANES], y[LANES:]
         h, l = split(jnp.concatenate([re * co - im * si, re * si + im * co], axis=0))
-        y = dot(inv_ref[0, c], h) + dot(inv_ref[0, c], l) + dot(inv_ref[1, c], h)
+        y = dot_tn(fwd_ref[0, c], h) + dot_tn(fwd_ref[0, c], l) + dot_tn(fwd_ref[1, c], h)
+        y = y * (1.0 / total)
         back.append((y[:LANES], y[LANES:]))
     half = PATCH // 2
     for a, pair in enumerate(fft_list(back, 1.0)):
@@ -174,9 +183,9 @@
 
 
 def focus_body(
-    names, sizes, valid_ref, root_ref, echo_ref, filt_ref, tw_ref, rf_ref, ri_ref,
-    slope_ref, centre_ref, af_ref, ai_ref, sel_ref,
-    image_ref, left_ref, right_ref, prime_ref,
+    names, sizes, valid_ref, root_ref, echo_ref, filt_ref, tw_ref, rf_ref,
+    slope_ref, centre_ref, af_ref, sel_ref, off_ref, fr_ref, fl_ref, il_ref, ones_ref,
+    out_ref, image_ref, left_ref, right_ref, padded, stack, power,
     zh, zl, comp, turned, crop, pass_up, pass_down, from_up, from_down,
     send_sem, recv_sem, halo_send, halo_recv, up_send, up_recv, down_send, down_recv,
 ):
@@ -243,7 +252,7 @@
     def compress(b, carry):
         r0 = pl.multiple_of(b * block, block)
         range_block(
-            r0, block, me * rows, valid_ref[0], echo_ref, filt_ref, tw_ref, rf_ref, ri_ref,
+            r0, block, me * rows, valid_ref[0], echo_ref, filt_ref, tw_ref, rf_ref,
             comp, zh, zl,
         )
         own = pl.ds(pl.multiple_of(me * cols, wide), cols)
@@ -319,37 +328,149 @@
             crop[j, q, PATCH * a : PATCH * a + PATCH, :] = value
 
         azimuth_block(
-            pl.multiple_of(j * wide, wide), turned, slope_ref, centre_ref, af_ref, ai_ref,
+            pl.multiple_of(j * wide, wide), turned, slope_ref, centre_ref, af_ref,
             sel_ref, image_ref, keep,
         )
         forward(j)
+
+        @pl.when(jnp.logical_and(j == 0, me > 0))
+        def _():
+            to_left.start()
+
         return carry
 
     lax.fori_loop(0, parts, focus, 0)
-
-    @pl.when(me > 0)
-    def _():
-        to_left.start()
 
     @pl.when(me < peers - 1)
     def _():
         to_right.start()
 
-    lax.fori_loop(parts, parts + stack_size - 1, lambda t, x: (forward(t), x)[1], 0)
-    for j in range(parts):
-        prime_ref[:, :, LANES * j : LANES * j + LANES] = jnp.where(
-            mine, crop[j], jnp.where(root_ref[0] < spot, from_up[j], from_down[j])
-        )
-
-    @pl.when(me > 0)
-    def _():
-        to_left.wait_send()
-        to_right.wait_recv()
-
-    @pl.when(me < peers - 1)
-    def _():
-        to_right.wait_send()
-        to_left.wait_recv()
+    total = image_ref.shape[1]
+    half = PATCH // 2
+    row_blocks = total // LANES
+    count = row_blocks * parts
+    def pad():
+        for q in range(2):
+            padded[q, :half, :] = jnp.zeros((half, cols + 2 * LANES), bf16)
+            padded[q, half + total :, :] = jnp.zeros((half, cols + 2 * LANES), bf16)
+            padded[q, half : half + total, LANES : LANES + cols] = image_ref[q]
+
+    def one_hot(condition):
+        return jnp.where(condition, 1.0, 0.0).astype(bf16)
+
+    def pair_window(i, jp):
+        base = pl.multiple_of(LANES * i, LANES)
+        picked, places = [], []
+        for s in range(2):
+            j = 2 * jp + s
+            row = PATCH + off_ref[0, 0, i, j]
+            col = LANES + half + off_ref[0, 1, i, j] - PATCH * s
+            m = lax.broadcasted_iota(jnp.int32, (PATCH, 3 * PATCH), 0)
+            r = lax.broadcasted_iota(jnp.int32, (PATCH, 3 * PATCH), 1)
+            rows_of = one_hot(r - m == row)
+            picked.append(jnp.concatenate([
+                dot(
+                    rows_of,
+                    padded[q, pl.ds(base, 3 * PATCH), LANES * j : LANES * j + 3 * LANES],
+                ).astype(bf16)
+                for q in range(2)
+            ], axis=0))
+            c = lax.broadcasted_iota(jnp.int32, (3 * LANES, LANES), 0)
+            n = lax.broadcasted_iota(jnp.int32, (3 * LANES, LANES), 1)
+            side = (n < PATCH) if s == 0 else (n >= PATCH)
+            places.append(one_hot(jnp.logical_and(c - n == col, side)))
+        both = dot(picked[0], places[0]) + dot(picked[1], places[1])
+        return both[:PATCH], both[PATCH:]
+
+    def put(n, pair):
+        at = pl.ds(pl.multiple_of(PATCH * n, PATCH), PATCH)
+        for q in range(2):
+            stack[at, LANES * q : LANES * q + LANES] = pair[q].astype(bf16)
+        re, im = pair[0].astype(f32), pair[1].astype(f32)
+        power[pl.ds(n, 1), :] = jnp.sum(re * re + im * im, axis=0, keepdims=True)
+
+    def windows():
+        @pl.when(me > 0)
+        def _():
+            to_left.wait_send()
+            to_right.wait_recv()
+
+        @pl.when(me < peers - 1)
+        def _():
+            to_right.wait_send()
+            to_left.wait_recv()
+
+        for q in range(2):
+            padded[q, half : half + total, :LANES] = left_ref[q]
+            padded[q, half : half + total, LANES + cols :] = right_ref[q]
+
+        def row_of(i, carry):
+            for jp in range(parts):
+                pair = pair_window(i, jp)
+                put(count + i * parts + jp, pair)
+            return carry
+
+        lax.fori_loop(0, row_blocks, row_of, 0)
+
+    def left(m_ref, value):
+        h, l = split(value)
+        return dot(m_ref[0], h) + dot(m_ref[0], l) + dot(m_ref[1], h)
+
+    def spectrum(start):
+        data = stack[PATCH * start : PATCH * (start + count)]
+        y = dot(data, fr_ref[0]) + dot(data, fr_ref[1])
+        return left(fl_ref, jnp.concatenate([
+            jnp.concatenate(
+                [y[PATCH * n : PATCH * n + PATCH, LANES * q : LANES * q + LANES] for n in range(count)],
+                axis=1,
+            )
+            for q in range(2)
+        ], axis=0))
+
+    work = [pad, windows]
+    for tick in range(stack_size - 1):
+        forward(parts + tick)
+        if work:
+            work.pop(0)()
+    for step in work:
+        step()
+    z = spectrum(count)
+    sr, si = z[:PATCH], z[PATCH:]
+    for i in range(row_blocks):
+        for jp in range(parts):
+            at = slice(PATCH * i, PATCH * i + PATCH)
+            put(i * parts + jp, [
+                jnp.where(
+                    mine, crop[jp, q, at],
+                    jnp.where(root_ref[0] < spot, from_up[jp, q, at], from_down[jp, q, at]),
+                )
+                for q in range(2)
+            ])
+    z = spectrum(0)
+    pr, pi = z[:PATCH], z[PATCH:]
+    x = left(il_ref, jnp.concatenate([pr * sr + pi * si, pi * sr - pr * si], axis=0))
+    x = jnp.concatenate([
+        jnp.concatenate(
+            [x[PATCH * q : PATCH * q + PATCH, LANES * n : LANES * n + LANES] for n in range(count)],
+            axis=0,
+        )
+        for q in range(2)
+    ], axis=1)
+    h, l = split(x)
+    y = dot_nt(h, fr_ref[0]) + dot_nt(l, fr_ref[0]) + dot_nt(h, fr_ref[1])
+    means = jnp.dot(
+        power[...], ones_ref[...], precision=lax.Precision.HIGHEST, preferred_element_type=f32
+    )
+    scale = lax.rsqrt(means + eps)
+    factor = scale[:count] * scale[count:] * (1.0 / PATCH**3)
+    for i in range(row_blocks):
+        for jp in range(parts):
+            n = i * parts + jp
+            part = y[PATCH * n : PATCH * n + PATCH]
+            for q in range(2):
+                out_ref[
+                    0, q, PATCH * i : PATCH * i + PATCH, LANES * jp : LANES * jp + LANES
+                ] = part[:, LANES * q : LANES * q + LANES] * factor[n : n + 1, :]
 
     for depth, opening, ending, buffer, staged, sends, recvs, step in lanes:
 
@@ -367,7 +488,7 @@
     lax.fori_loop(0, parts, finish, 0)
 
 
-def focus(names, sizes, valid, root, echo, filt, slope, centre):
+def focus(names, sizes, valid, root, echo, filt, slope, centre, offsets):
     rows, length = echo.shape[2:]
     lead = length // LANES
     block = min(rows, 32)
@@ -377,35 +498,40 @@
     wide = 2 * LANES
     parts = cols // wide
     rf = halves(right_form(dft(LANES, -1.0)))
-    ri = halves(right_form(dft(LANES, 1.0)))
     angle = 2 * np.pi * np.outer(np.arange(lead), np.arange(LANES)) / length
     tw = np.stack([np.cos(angle), -np.sin(angle)]).astype(np.float32)
     filt = filt[0].reshape(2, LANES, lead).transpose(0, 2, 1) * (1.0 / length)
-    fwd, inv = [], []
+    fwd = []
     for c in range(total // LANES):
         phase = np.exp(-2j * np.pi * c * np.arange(LANES) / total)
         fwd.append(left_form(dft(LANES, -1.0) * phase[None, :]))
-        inv.append(left_form(dft(LANES, 1.0) * phase.conj()[:, None] / total))
-    fwd, inv = halves(np.stack(fwd)), halves(np.stack(inv))
+    fwd = halves(np.stack(fwd))
     sel = np.zeros((wide, LANES), np.float32)
     lane = np.arange(PATCH)
     sel[lane + PATCH // 2, lane] = 1
     sel[lane + LANES + PATCH // 2, lane + PATCH] = 1
     sel = sel.astype(bf16)
+    count = (total // LANES) * parts
+    two = np.eye(2)
+    fr = halves(right_form(np.kron(two, dft(PATCH, -1.0))))
+    fl = halves(left_form(dft(PATCH, -1.0)))
+    il = halves(left_form(dft(PATCH, 1.0)))
+    ones = np.kron(two, np.full((PATCH, PATCH), 1.0 / PATCH**2)).astype(np.float32)
     smem, vmem = pl.BlockSpec(memory_space=pltpu.SMEM), pl.BlockSpec(memory_space=pltpu.VMEM)
     dma = pltpu.SemaphoreType.DMA
     chunk = pltpu.VMEM((parts, 2, total // 2, LANES), bf16)
     return pl.pallas_call(
         functools.partial(focus_body, names, sizes),
-        in_specs=[smem] * 2 + [vmem] * 10,
-        out_specs=[vmem] * 4,
-        out_shape=[
-            jax.ShapeDtypeStruct((2, total, cols), bf16),
-            jax.ShapeDtypeStruct((2, total, LANES), bf16),
-            jax.ShapeDtypeStruct((2, total, LANES), bf16),
-            jax.ShapeDtypeStruct((2, total // 2, cols // 2), bf16),
-        ],
+        in_specs=[smem] * 2 + [vmem] * 8 + [smem] + [vmem] * 4,
+        out_specs=vmem,
+        out_shape=jax.ShapeDtypeStruct((1, 2, total // 2, cols // 2), f32),
         scratch_shapes=[
+            pltpu.VMEM((2, total, cols), bf16),
+            pltpu.VMEM((2, total, LANES), bf16),
+            pltpu.VMEM((2, total, LANES), bf16),
+            pltpu.VMEM((2, total + PATCH, cols + 2 * LANES), bf16),
+            pltpu.VMEM((2 * count * PATCH, 2 * LANES), bf16),
+            pltpu.VMEM((2 * count, LANES), f32),
             pltpu.VMEM((lead * block, wide), bf16),
             pltpu.VMEM((lead * block, wide), bf16),
             pltpu.VMEM((2, rows, length), bf16),
@@ -417,130 +543,11 @@
         + [dma((parts,))] * 4,
         compiler_params=pltpu.CompilerParams(collective_id=0, has_side_effects=True),
         name="focus",
-    )(valid, root, echo, filt, tw, rf, ri, slope, centre, fwd, inv, sel)
-
-
-def correlate_body(
-    off_ref, image_ref, left_ref, right_ref, crop_ref, fr_ref, fl_ref, ir_ref, il_ref, ones_ref,
-    out_ref, padded, stack, high, low, power,
-):
-    total, cols = image_ref.shape[1:]
-    half = PATCH // 2
-    row_blocks, pairs = total // LANES, cols // (2 * LANES)
-    count = row_blocks * pairs
-    for q in range(2):
-        padded[q, :half, :] = jnp.zeros((half, cols + 3 * LANES), f32)
-        padded[q, half + total :, :] = jnp.zeros((half + 8, cols + 3 * LANES), f32)
-        padded[q, half : half + total, :LANES] = left_ref[q].astype(f32)
-        padded[q, half : half + total, LANES : LANES + cols] = image_ref[q].astype(f32)
-        padded[q, half : half + total, LANES + cols : 2 * LANES + cols] = right_ref[q].astype(f32)
-    lane = lax.broadcasted_iota(jnp.int32, (1, LANES), 1)
-
-    def window(q, i, j, target):
-        row = LANES * i + PATCH + off_ref[0, 0, i, j]
-        col = LANES * j + LANES + half + off_ref[0, 1, i, j]
-        base = pl.multiple_of(col // LANES * LANES, LANES)
-        offset = col - base
-        shift = (target - offset + LANES) % LANES
-        top = pl.multiple_of(row // 8 * 8, 8)
-        first = padded[q, pl.ds(top, PATCH + 8), pl.ds(base, LANES)]
-        second = padded[q, pl.ds(top, PATCH + 8), pl.ds(pl.multiple_of(base + LANES, LANES), LANES)]
-        first = pltpu.roll(first, shift, 1)
-        second = pltpu.roll(second, shift, 1)
-        joined = jnp.where(lane + offset - target < LANES, first, second)
-        return pltpu.roll(joined, (PATCH + 8 - (row - top)) % (PATCH + 8), 0)[:PATCH]
-
-    def total_of(re, im):
-        return jnp.sum(re * re + im * im, axis=0, keepdims=True)
-
-    for i in range(row_blocks):
-        for jp in range(pairs):
-            n = i * pairs + jp
-            parts = [
-                jnp.where(lane < PATCH, window(q, i, 2 * jp, 0), window(q, i, 2 * jp + 1, PATCH))
-                for q in range(2)
-            ]
-            power[count + n : count + n + 1, :] = total_of(*parts)
-            prime = [
-                crop_ref[q, PATCH * i : PATCH * i + PATCH, LANES * jp : LANES * jp + LANES]
-                for q in range(2)
-            ]
-            power[n : n + 1, :] = total_of(prime[0].astype(f32), prime[1].astype(f32))
-            for q in range(2):
-                stack[PATCH * n : PATCH * n + PATCH, LANES * q : LANES * q + LANES] = prime[q]
-                at = PATCH * (count + n)
-                stack[at : at + PATCH, LANES * q : LANES * q + LANES] = parts[q].astype(bf16)
-
-    y = dot(stack[...], fr_ref[0]) + dot(stack[...], fr_ref[1])
-    for n in range(2 * count):
-        part = y[PATCH * n : PATCH * n + PATCH]
-        for q in range(2):
-            h, l = split(part[:, LANES * q : LANES * q + LANES])
-            high[PATCH * q : PATCH * q + PATCH, LANES * n : LANES * n + LANES] = h
-            low[PATCH * q : PATCH * q + PATCH, LANES * n : LANES * n + LANES] = l
-
-    def left(m_ref, h, l):
-        return dot(m_ref[0], h) + dot(m_ref[0], l) + dot(m_ref[1], h)
-
-    z = left(fl_ref, high[...], low[...])
-    wide = count * LANES
-    pr, pi, sr, si = z[:PATCH, :wide], z[PATCH:, :wide], z[:PATCH, wide:], z[PATCH:, wide:]
-    cross = jnp.concatenate([pr * sr + pi * si, pi * sr - pr * si], axis=0)
-    x = left(il_ref, *split(cross))
-    for n in range(count):
-        for q in range(2):
-            h, l = split(x[PATCH * q : PATCH * q + PATCH, LANES * n : LANES * n + LANES])
-            stack[PATCH * n : PATCH * n + PATCH, LANES * q : LANES * q + LANES] = h
-            at = PATCH * (count + n)
-            stack[at : at + PATCH, LANES * q : LANES * q + LANES] = l
-    h, l = stack[: PATCH * count], stack[PATCH * count :]
-    y = dot(h, ir_ref[0]) + dot(l, ir_ref[0]) + dot(h, ir_ref[1])
-    means = jnp.dot(
-        power[...], ones_ref[...], precision=lax.Precision.HIGHEST, preferred_element_type=f32
-    )
-    scale = lax.rsqrt(means + eps)
-    factor = scale[:count] * scale[count:] * (1.0 / PATCH**3)
-    for i in range(row_blocks):
-        for jp in range(pairs):
-            n = i * pairs + jp
-            part = y[PATCH * n : PATCH * n + PATCH]
-            for q in range(2):
-                out_ref[
-                    0, q, PATCH * i : PATCH * i + PATCH, LANES * jp : LANES * jp + LANES
-                ] = part[:, LANES * q : LANES * q + LANES] * factor[n : n + 1, :]
-
-
-def correlate(offsets, image, left, right, crop):
-    total, cols = image.shape[1:]
-    count = (total // LANES) * (cols // (2 * LANES))
-    two = np.eye(2)
-    fr = halves(right_form(np.kron(two, dft(PATCH, -1.0))))
-    ir = halves(right_form(np.kron(two, dft(PATCH, 1.0))))
-    fl = halves(left_form(dft(PATCH, -1.0)))
-    il = halves(left_form(dft(PATCH, 1.0)))
-    ones = np.kron(two, np.full((PATCH, PATCH), 1.0 / PATCH**2)).astype(np.float32)
-    vmem = pl.BlockSpec(memory_space=pltpu.VMEM)
-    return pl.pallas_call(
-        correlate_body,
-        in_specs=[pl.BlockSpec(memory_space=pltpu.SMEM)] + [vmem] * 9,
-        out_specs=vmem,
-        out_shape=jax.ShapeDtypeStruct((1, 2, total // 2, cols // 2), f32),
-        scratch_shapes=[
-            pltpu.VMEM((2, total + PATCH + 8, cols + 3 * LANES), f32),
-            pltpu.VMEM((2 * count * PATCH, 2 * LANES), bf16),
-            pltpu.VMEM((2 * PATCH, 2 * count * LANES), bf16),
-            pltpu.VMEM((2 * PATCH, 2 * count * LANES), bf16),
-            pltpu.VMEM((2 * count, LANES), f32),
-        ],
-        name="correlate",
-    )(offsets, image, left, right, crop, fr, fl, ir, il, ones)
+    )(valid, root, echo, filt, tw, rf, slope, centre, fwd, sel, offsets, fr, fl, il, ones)
 
 
 def on_device(names, sizes, echo, filt, slope, centre, valid, reference_index, offsets):
-    image, left, right, primary = focus(
-        names, sizes, valid, reference_index, echo, filt, slope, centre
-    )
-    return correlate(offsets, image, left, right, primary)
+    return focus(names, sizes, valid, reference_index, echo, filt, slope, centre, offsets)
 
 
 def solution(mesh):

time: 69.1 us -> 65.3 us (0.945)
  Pallas kernels: 66 us -> 59.9 us
  local copies, waits for them, and re-layouts: 0.81 us -> 3.07 us
    pallas_call x1 -> x0, Pallas kernels: 8.4 us -> none  [correlate(): pl.pallas_call(correlate_body, in_specs=[pl.BlockSpec(memory_space=pltpu....]
    pallas_call x1, Pallas kernels: 57.6 us -> 59.9 us  [focus(): pl.pallas_call(functools.partial(focus_body, names, sizes), in_specs=[sme...]
    unnamed x0 -> x1, local copies, waits for them, and re-layouts: none -> 2.26 us
where the time goes in v2:
time: 65.3 us; the launch traced here: 65.1 us
  Pallas kernels  59.9 us (92%)
  local copies, waits for them, and re-layouts  3.07 us (5%)
  between operations  1.32 us (2%)
  other arithmetic  0.77 us (1%)
    pallas_call x1, Pallas kernels, focus(): pl.pallas_call(functools.partial(focus_body, names, sizes), in_specs=[sme...  59.9 us
    unnamed x1, local copies, waits for them, and re-layouts  2.26 us

profile of v2, /device:TPU:0, one launch (start us, length us, event | category | flops | bytes accessed | tf_op | source)
XLA Modules:
  0.0 65.1 jit_solution(5544452300358859929)
XLA Ops:
  1.3 0.8 %broadcast_multiply_fusion = f32[1,2,4096]{2,1,0:T(2,128)S(1)} fusion(f32[1,2,4096]{2,1,0:T(2,128)} %param.16), kind=kLoop, calls=%fused_computation | loop fusion | flops 8192 | bytes 65536 | tf_op jit(solution)/shard_map/mul | solution.py:503
  2.1 0.1 mul.12
  2.2 0.7 %copy.16 = f32[2,128,32]{1,2,0:T(8,128)} copy(f32[2,128,32]{2,1,0:T(8,128)S(1)} %mul.12) | data formatting | bytes 65536 | tf_op jit(solution)/shard_map/mul | solution.py:503
  2.9 59.9 %focus.1 = f32[1,2,256,512]{3,2,1,0:T(8,128)} custom-call(s32[1]{0:T(128)S(6)} %copy.18.valid_ref, s32[1]{0:T(128)S(6)} %copy.19.root_ref, bf16[1,2,128,4096]{3,2,1,0:T(8,128)(2,1)} %echo_ref.1, f32[2,32,128]{2,1,0:T(8,128)} %bitcast.1, f32[2,32,128]{2,1,0:T(8,128)} %constant.18.clone.tw_ref, bf16[2,256,256]{2,1,0:T(8,128)(2,1)} %constant.19.clone.rf_ref, ...), custom_call_target="tpu_custom_call" | custom-call | tf_op jit(solution)/shard_map/focus/pallas_call | solution.py:523
  62.8 2.3 %copy.20 = f32[1,2,256,512]{3,2,1,0:T(8,128)} copy(f32[1,2,256,512]{3,2,1,0:T(8,128)} %focus.1) | data formatting | bytes 2097152
